TPU v7x, 256 devices: a whole 4x4x8 slice. The times are simulated.
256 devices in a mesh: slab: 64 (over z, x, core), dom: 4 (over y).
Axes of the slice: x: 4, y: 4, z: 8, core: 2. Of those that a mesh axis runs over, the one named last changes fastest.
Arguments:
- elem_grad: float32 [3, 8, 1376256], P(None, None, ('slab', 'dom')), may hold values from -3 to 3
- elem_stress: float32 [6, 1376256], P(None, ('slab', 'dom')), may hold values from -6 to 6
- elem_grade: int32 [1376256], P(('slab', 'dom')), may hold values from 0 to 15
- grade_scale: float32 [16], replicated, may hold values from 0.5 to 2
- part_counts: int32 [64, 4], P('slab'), may hold values from 1 to 5376, as said below
- node_lists: int32 [4, 128, 8, 512], P(None, 'slab', None, 'dom'), may hold values from -1 to 7167, as said below
- stiff_diag: float32 [3, 128, 8, 512], P(None, 'slab', None, 'dom'), may hold values from 1 to 4
- start_block: float32 [3, 32, 128, 8, 512], P(None, None, 'slab', None, 'dom'), may hold values from -600 to 600
Outputs:
- next_block: float32 [3, 32, 128, 8, 512], P(None, None, 'slab', None, 'dom')
- diag_blocks: float32 [2, 32, 32], replicated
- offdiag_blocks: float32 [3, 32, 32], replicated
Inputs may be any that keep to these rules, and one draw needn't show every extreme that they name: `part_counts`: each row sums to 7168, the elements of one slab; in every slab one partition holds exactly 5376. node_lists[j, f, x, y] is the pool number, within the slab of floor f, of the element of layer f whose in-plane base corner is (x - j mod 2, (y - j // 2) mod 512); it is -1 exactly where x - j mod 2 lies outside 0 to 6. Every element of a slab appears at its four in-plane corners.
All inputs are finite; a program needn't handle non-finite values.
Results may differ from a plain program's by a relative error of at most 0.0003.
Values sent between devices are 32-bit elements; how exact they have to be, the bound alone decides.
No kernel may reach another device: no remote copies, remote signals or barrier semaphores. Data moves between devices by JAX's collectives and lax.ppermute only.
A program may use at most 128 MiB of HBM per device.

v0:
```python
import jax
import jax.numpy as jnp
import numpy as np
from jax import lax
from jax.sharding import PartitionSpec as P

highest = lax.Precision.HIGHEST


def extended_2(cells, sides, width):
    for axis, dim in sides:
        count = lax.axis_size(axis)
        ends = count - 1
        head = lax.slice_in_dim(cells, 0, width, axis=dim)
        tail = lax.slice_in_dim(cells, cells.shape[dim] - width, cells.shape[dim], axis=dim)
        cells = jnp.concatenate(
            [
                lax.ppermute(tail, axis, [(i, (i + 1) % count) for i in range(ends)]),
                cells,
                lax.ppermute(head, axis, [((i + 1) % count, i) for i in range(ends)]),
            ],
            axis=dim,
        )
    return cells


def from_behind(value, axis, steps):
    count = lax.axis_size(axis)
    pairs = [(source, (source + steps) % count) for source in range(count)]
    return lax.ppermute(value, axis, pairs)


def passed_along(block, axis, distance):
    devices = range(lax.axis_size(axis))
    route = [(i - distance, i) for i in devices if i - distance in devices]
    return lax.ppermute(block, axis, route)


def offset_table(quad_slot, layer_side):
    table = np.zeros((8, 27))
    shift_x = quad_slot % 2
    shift_y = quad_slot // 2
    for corner in range(8):
        corner_x = corner % 2
        corner_y = corner // 2 % 2
        corner_z = corner // 4
        target = (
            corner_x - shift_x + 1 + 3 * (corner_y - shift_y + 1) + 9 * (corner_z - layer_side + 1)
        )
        table[corner, target] = 1.0
    return jnp.asarray(table, dtype=jnp.float32)


def stress_matrix(stress):
    return jnp.stack(
        [
            jnp.stack([stress[0], stress[5], stress[4]]),
            jnp.stack([stress[5], stress[1], stress[3]]),
            jnp.stack([stress[4], stress[3], stress[2]]),
        ]
    )


def grade_lookup(grades, table):
    levels = jnp.arange(table.shape[0], dtype=jnp.int32)[:, None]
    onehot = (grades[None, :] == levels).astype(jnp.float32)
    return jnp.dot(table, onehot, precision=highest)


def element_matrices(gradients, stress, scales):
    pushed = jnp.einsum("ik...,kb...->ib...", stress_matrix(stress), gradients, precision=highest)
    return jnp.einsum("ia...,ib...->ab...", gradients, pushed, precision=highest) * scales


def pool_columns(slot_lists, counts, capacity):
    offsets = jnp.cumsum(counts) - counts
    shaped = offsets.reshape((-1,) + (1,) * slot_lists.ndim)
    pool_ids = jnp.maximum(slot_lists, 0)
    partition = jnp.sum((pool_ids[None] >= shaped[1:]).astype(jnp.int32), axis=0)
    levels = jnp.arange(counts.shape[0], dtype=jnp.int32).reshape(shaped.shape)
    starts = jnp.sum(jnp.where(partition[None] == levels, shaped, 0), axis=0)
    columns = partition * capacity + pool_ids - starts
    return (columns, (slot_lists >= 0).astype(jnp.float32))


def accumulate(getter, present):
    sides = []
    for layer_side in range(2):
        summed = None
        for quad_slot in range(4):
            row_values = getter(quad_slot, layer_side) * present[quad_slot]
            contribution = jnp.einsum(
                "bfxy,bo->ofxy", row_values, offset_table(quad_slot, layer_side), precision=highest
            )
            summed = contribution if summed is None else summed + contribution
        sides.append(summed)
    return (sides[0], sides[1])


def apply_operator(block, stencil, diagonal):
    extended = extended_2(block, (("slab", 2),), 1)
    edge_shape = extended.shape[:4]
    first_column = extended[..., 0].reshape(-1)
    last_column = extended[..., -1].reshape(-1)
    from_left = from_behind(last_column, "dom", 1).reshape(edge_shape + (1,))
    from_right = from_behind(first_column, "dom", -1).reshape(edge_shape + (1,))
    extended = jnp.concatenate([from_left, extended, from_right], axis=4)
    padded = jnp.pad(extended, ((0, 0), (0, 0), (0, 0), (1, 1), (0, 0)))
    floors, across, beside_all = (block.shape[2], block.shape[3], block.shape[4])
    result = diagonal[:, None] * block
    for offset in range(27):
        step_x = offset % 3
        step_y = offset // 3 % 3
        step_z = offset // 9
        result = (
            result
            + stencil[offset]
            * padded[
                :,
                :,
                step_z : step_z + floors,
                step_x : step_x + across,
                step_y : step_y + beside_all,
            ]
        )
    return result


def local_inner(first_block, second_block):
    return jnp.einsum("cvfxy,cwfxy->vw", first_block, second_block, precision=highest)


def mix(block, matrix):
    return jnp.einsum("cvfxy,vw->cwfxy", block, matrix, precision=highest)


def normalize(block, gram_matrix):
    factor = jnp.linalg.cholesky(gram_matrix)
    identity = jnp.eye(gram_matrix.shape[0], dtype=jnp.float32)
    inverse = lax.linalg.triangular_solve(factor, identity, left_side=True, lower=True)
    return (jnp.einsum("cvfxy,wv->cwfxy", block, inverse, precision=highest), factor.T)


def advance(basis_block, image_block, dof_count):
    projection = lax.psum(local_inner(basis_block, image_block), ("slab", "dom")) / dof_count
    residual = image_block - mix(basis_block, projection)
    gram_matrix = lax.psum(local_inner(residual, residual), ("slab", "dom")) / dof_count
    following, upper_factor = normalize(residual, gram_matrix)
    return (following, projection, upper_factor)


def per_device(
    elem_grad,
    elem_stress,
    elem_grade,
    grade_scale,
    part_counts,
    node_lists,
    stiff_diag,
    start_block,
):
    capacity = elem_grad.shape[2]
    counts = part_counts[0]
    columns, present = pool_columns(node_lists, counts, capacity)
    flat_columns = columns.reshape(-1)
    slot_shape = node_lists.shape
    scales = grade_lookup(elem_grade, grade_scale)
    matrices = element_matrices(elem_grad, elem_stress, scales).reshape(64, capacity)
    shard_piece = lax.all_gather(matrices, "dom", axis=1, tiled=True)
    inside = (flat_columns >= 0) & (flat_columns < shard_piece.shape[1])
    selected = jnp.take(shard_piece, jnp.clip(flat_columns, 0, shard_piece.shape[1] - 1), axis=1)
    picked = jnp.where(inside[None, :], selected, 0.0)
    picked = picked.reshape((8, 8) + slot_shape)

    def getter(quad_slot, layer_side):
        return picked[quad_slot + 4 * layer_side, :, quad_slot]

    bottom, top_side = accumulate(getter, present)
    below = passed_along(bottom[:, 0], "slab", -1)
    stencil = top_side + jnp.concatenate([bottom[:, 1:], below[:, None]], axis=1)
    dof_count = (
        3
        * start_block.shape[2]
        * start_block.shape[3]
        * start_block.shape[4]
        * lax.axis_size("slab")
        * lax.axis_size("dom")
    )
    start_gram = lax.psum(local_inner(start_block, start_block), ("slab", "dom")) / dof_count
    first, start_factor = normalize(start_block, start_gram)
    image_block = apply_operator(first, stencil, stiff_diag)
    second, alpha_one, beta_one = advance(first, image_block, dof_count)
    image_block = apply_operator(second, stencil, stiff_diag) - mix(first, beta_one.T)
    third, alpha_two, beta_two = advance(second, image_block, dof_count)
    return (third, jnp.stack([alpha_one, alpha_two]), jnp.stack([start_factor, beta_one, beta_two]))


def solution(mesh):
    in_specs = (
        P(None, None, ("slab", "dom")),
        P(None, ("slab", "dom")),
        P(("slab", "dom")),
        P(),
        P("slab", None),
        P(None, "slab", None, "dom"),
        P(None, "slab", None, "dom"),
        P(None, None, "slab", None, "dom"),
    )
    out_specs = (P(None, None, "slab", None, "dom"), P(), P())
    return jax.shard_map(
        per_device, mesh=mesh, in_specs=in_specs, out_specs=out_specs, check_vma=False
    )
```

profile of v0, /device:TPU:1, one launch (start us, length us, event | category | flops | bytes accessed | tf_op | source)
XLA Modules:
  0.0 704.9 jit_solution(14707492040384633531)
XLA Ops:
  9.1 7.5 %copy.136 = f32[3,3,5376]{1,0,2:T(4,128)} copy(f32[3,3,5376]{2,1,0:T(4,128)S(1)} %pad_maximum_fusion.18) | data formatting | bytes 387072 | tf_op jit(solution)/shard_map/stack | solution.py:55
  16.6 7.2 %copy.137 = f32[3,8,5376]{1,0,2:T(4,128)} copy(f32[3,8,5376]{2,1,0:T(8,128)S(1)} %copy-done.12) | data formatting | bytes 1032192 | tf_op args[0]
  23.9 39.3 %fusion.144 = f32[5376,3,8]{2,1,0:T(4,128)S(1)} fusion(f32[3,3,5376]{1,0,2:T(4,128)} %copy.136, f32[3,8,5376]{1,0,2:T(4,128)} %copy.137), kind=kOutput, calls=%fused_computation.282 | convolution fusion | flops 4644864 | bytes 1225728 | tf_op jit(solution)/shard_map/ik...,kb...->ib.../dot_general | solution.py:71
  63.5 57.4 %multiply_bitcast_fusion = f32[8,8,5376]{0,1,2:T(8,128)} fusion(f32[5376]{0:T(1024)S(1)} %convolution_reduce_fusion, f32[3,8,5376]{1,0,2:T(4,128)S(1)} %copy-done.2, f32[5376,3,8]{2,1,0:T(4,128)S(1)} %fusion.144), kind=kOutput, calls=%fused_computation.1 | convolution fusion | flops 12730368 | bytes 2429952 | tf_op jit(solution)/shard_map/ia...,ib...->ab.../dot_general | solution.py:72
  120.9 12.2 %copy.139 = f32[8,8,5376]{2,1,0:T(8,128)S(1)} copy(f32[8,8,5376]{0,1,2:T(8,128)} %multiply_bitcast_fusion) | data formatting | bytes 2752512 | tf_op jit(solution)/shard_map/mul | solution.py:72
  133.1 2.1 copy.140
  136.2 82.3 %psum.35 = f32[32,32]{0,1:T(8,128)S(1)} all-reduce(f32[32,32]{0,1:T(8,128)S(1)} %convolution_bitcast_fusion.10), channel_id=1, replica_groups=mesh['slab'=64,'dom'=4] {'slab','dom'}, use_global_device_ids=true, to_apply=%region_0.0 | all-reduce | flops 1024 | bytes 8192 | tf_op jit(solution)/shard_map/psum | solution.py:189
  218.5 2.9 cholesky.59
  223.4 2.4 custom-call.7
  227.1 2.2 collective-permute-start.1
  229.2 2.4 collective-permute-start.2
  233.9 4.8 collective-permute-done.2
  238.9 1.7 fusion.137
  240.6 3.8 copy.154
  244.9 2.4 copy.155
  247.5 2.5 collective-permute-start.4
  250.8 2.3 copy.156
  253.4 3.5 copy.157
  256.9 4.5 select_maximum_fusion.4
  261.4 31.8 %gather_fusion = f32[8192,64]{1,0:T(8,128)} fusion(f32[64,21504]{0,1:T(8,128)} %all-gather.2.cloned.1.call-done, s32[8192]{0:T(1024)S(1)} %copy-done.13), kind=kCustom, calls=%fused_computation | custom fusion | bytes 4227072 | tf_op jit(solution)/shard_map/jit(_take)/gather | solution.py:171
  293.2 3.8 copy.141
  297.1 2.0 copy.205
  301.3 2.3 collective-permute-start
  304.9 2.7 collective-permute-done
  308.5 5.3 fusion.41
  314.9 81.3 %psum.36 = f32[32,32]{0,1:T(8,128)S(1)} all-reduce(f32[32,32]{0,1:T(8,128)S(1)} %convolution_bitcast_fusion.9), channel_id=1, replica_groups=mesh['slab'=64,'dom'=4] {'slab','dom'}, use_global_device_ids=true, to_apply=%region_6.9 | all-reduce | flops 1024 | bytes 8192 | tf_op jit(solution)/shard_map/psum | solution.py:145
  397.7 73.5 %psum.37 = f32[32,32]{0,1:T(8,128)S(1)} all-reduce(f32[32,32]{0,1:T(8,128)S(1)} %convolution_bitcast_fusion.8), channel_id=1, replica_groups=mesh['slab'=64,'dom'=4] {'slab','dom'}, use_global_device_ids=true, to_apply=%region_7.10 | all-reduce | flops 1024 | bytes 8192 | tf_op jit(solution)/shard_map/psum | solution.py:147
  471.3 2.9 cholesky.70
  476.2 2.4 custom-call.8
  479.8 3.5 collective-permute-start.5
  483.3 1.9 collective-permute-start.6
  485.2 2.8 collective-permute-done.5
  488.0 4.4 collective-permute-done.6
  493.2 1.7 fusion.136
  495.0 4.4 copy.163
  499.4 1.7 reshape_squeeze.14
  501.3 3.0 copy.164
  504.3 1.7 reshape_squeeze.15
  506.0 2.7 collective-permute-start.8
  510.9 3.2 copy.165
  515.8 4.4 copy.166
  520.4 3.4 select_maximum_fusion
  524.1 7.2 %fusion.10 = f32[3,32,2,8,128]{4,1,3,2,0:T(8,128)S(1)} fusion(f32[3,32,4,10,130]{4,1,3,2,0:T(8,128)S(1)} %select_maximum_fusion, f32[3,32,4,8,1]{4,1,3,2,0:T(8,128)S(1)} %copy-done.5, f32[3,32,1,8,128]{4,1,3,2,0:T(8,128)S(1)} %copy-done.11, f32[3,32,2,8,128]{4,1,3,2,0:T(8,128)S(1)} %convolution_bitcast_fusion.3, ...), kind=kOutput, calls=%fused_computation.45 | convolution fusion | flops 90442752 | bytes 17575936 | tf_op jit(solution)/shard_map/cvfxy,vw->cwfxy/dot_general | solution.py:134
  533.0 78.2 %psum.38 = f32[32,32]{0,1:T(8,128)S(1)} all-reduce(f32[32,32]{0,1:T(8,128)S(1)} %convolution_bitcast_fusion.7), channel_id=1, replica_groups=mesh['slab'=64,'dom'=4] {'slab','dom'}, use_global_device_ids=true, to_apply=%region_8.11 | all-reduce | flops 1024 | bytes 8192 | tf_op jit(solution)/shard_map/psum | solution.py:145
  611.2 1.9 fusion.5
  613.9 73.4 %psum.39 = f32[32,32]{0,1:T(8,128)S(1)} all-reduce(f32[32,32]{0,1:T(8,128)S(1)} %convolution_bitcast_fusion.6), channel_id=1, replica_groups=mesh['slab'=64,'dom'=4] {'slab','dom'}, use_global_device_ids=true, to_apply=%region_9.12 | all-reduce | flops 1024 | bytes 8192 | tf_op jit(solution)/shard_map/psum | solution.py:147
  687.4 2.9 cholesky.81
  693.0 2.4 custom-call.9
  (268 shorter events, 32.7 us)
Async XLA Ops:
  7.2 56.1 %copy-start = (f32[16]{0:T(128)S(1)}, f32[16]{0:T(128)}, u32[]{:S(2)}) copy-start(f32[16]{0:T(128)} %param.22) | copy-start | bytes 196
  7.2 254.2 %all-gather.2.cloned.1.call-start = ((), (), s32[]{:S(2)}) async-start(), calls=%async_computation | async-start | bytes 13762560 | tf_op jit(solution)/shard_map/all_gather | solution.py:169
  9.1 7.5 %copy-start.12 = (f32[3,8,5376]{2,1,0:T(8,128)S(1)}, f32[3,8,5376]{2,1,0:T(8,128)}, u32[]{:S(2)}) copy-start(f32[3,8,5376]{2,1,0:T(8,128)} %param.19) | copy-start | bytes 1548292
  23.9 39.4 %copy-start.89 = (s32[5376]{0:T(1024)S(1)}, s32[5376]{0:T(1024)}, u32[]{:S(2)}) copy-start(s32[5376]{0:T(1024)} %param.21) | copy-start | bytes 64516
  23.9 39.6 %copy-start.2 = (f32[3,8,5376]{1,0,2:T(4,128)S(1)}, f32[3,8,5376]{1,0,2:T(4,128)}, u32[]{:S(2)}) copy-start(f32[3,8,5376]{1,0,2:T(4,128)} %copy.137) | copy-start | bytes 1548292
  135.2 96.4 %copy-start.90 = (s32[1,4]{1,0:T(1,128)S(1)}, s32[1,4]{1,0:T(1,128)}, u32[]{:S(2)}) copy-start(s32[1,4]{1,0:T(1,128)} %param.23) | copy-start | bytes 52
  135.2 96.7 %copy-start.14 = (s32[4,2,8,128]{3,2,1,0:T(8,128)S(1)}, s32[4,2,8,128]{3,2,1,0:T(8,128)}, u32[]{:S(2)}) copy-start(s32[4,2,8,128]{3,2,1,0:T(8,128)} %param.24) | copy-start | bytes 98308
  227.1 6.9 collective-permute-start.1
  229.2 9.5 %collective-permute-start.2 = (f32[3,32,1,8,128]{4,1,3,2,0:T(8,128)S(1)}, f32[3,32,1,8,128]{4,1,3,2,0:T(8,128)S(1)}, u32[]{:S(2)}, u32[]{:S(2)}) collective-permute-start(f32[3,32,1,8,128]{4,1,3,2,0:T(8,128)S(1)} %get-tuple-element.40), channel_id=1, source_target_pairs={{4,0},{8,4},{12,8},{16,12},{20,16},{24,20},{28,24},{32,28},{36,32}... | collective-permute-start | bytes 1179656 | tf_op jit(solution)/shard_map/ppermute | solution.py:20
  238.7 18.1 %copy-start.6 = (f32[3,32,1,8,128]{4,1,3,2,0:T(8,128)}, f32[3,32,1,8,128]{4,1,3,2,0:T(8,128)S(1)}, u32[]{:S(2)}) copy-start(f32[3,32,1,8,128]{4,1,3,2,0:T(8,128)S(1)} %collective-permute-done.2) | copy-start | bytes 1179652
  238.8 11.1 %copy-start.15 = (f32[4,2,8,128]{3,2,1,0:T(8,128)S(1)}, f32[4,2,8,128]{3,2,1,0:T(8,128)}, u32[]{:S(2)}) copy-start(f32[4,2,8,128]{3,2,1,0:T(8,128)} %get-tuple-element.80) | copy-start | bytes 98308
  244.5 6.0 collective-permute-start.3
  247.5 5.7 collective-permute-start.4
  293.2 5.9 copy-start.78
  299.2 8.4 %copy-start.81 = (f32[8,27,1,1]{1,0,3,2:T(8,128)S(1)}, f32[8,27,1,1]{1,0,3,2:T(8,128)}, u32[]{:S(2)}) copy-start(f32[8,27,1,1]{1,0,3,2:T(8,128)} %constant.100) | copy-start | bytes 2596
  299.4 9.0 %copy-start.3 = (f32[3,32,4,10,130]{4,1,3,2,0:T(8,128)S(1)}, f32[3,32,4,10,130]{4,1,3,2,0:T(8,128)}, u32[]{:S(2)}) copy-start(f32[3,32,4,10,130]{4,1,3,2,0:T(8,128)} %select_maximum_fusion.4) | copy-start | bytes 5990404
  299.4 9.0 %copy-start.4 = (f32[3,32,4,8,1]{4,1,3,2,0:T(8,128)S(1)}, f32[3,32,4,8,1]{4,1,3,2,0:T(8,128)}, u32[]{:S(2)}) copy-start(f32[3,32,4,8,1]{4,1,3,2,0:T(8,128)} %copy.157) | copy-start | bytes 36868
  299.5 9.0 %copy-start.7 = (f32[3,32,1,8,128]{4,1,3,2,0:T(8,128)S(1)}, f32[3,32,1,8,128]{4,1,3,2,0:T(8,128)}, u32[]{:S(2)}) copy-start(f32[3,32,1,8,128]{4,1,3,2,0:T(8,128)} %copy-done.6) | copy-start | bytes 1179652
  299.5 9.0 %copy-start.79 = (f32[3,2,8,128]{3,2,1,0:T(8,128)S(1)}, f32[3,2,8,128]{3,2,1,0:T(8,128)}, u32[]{:S(2)}) copy-start(f32[3,2,8,128]{3,2,1,0:T(8,128)} %param.25) | copy-start | bytes 73732
  301.3 6.3 collective-permute-start
  308.1 5.7 copy-start.21
  308.1 5.7 copy-start.23
  308.1 5.7 copy-start.25
  308.1 5.7 copy-start.27
  308.1 5.7 copy-start.29
  308.1 5.7 copy-start.31
  308.1 5.7 copy-start.33
  308.2 5.7 copy-start.35
  308.2 5.7 copy-start.37
  308.2 5.7 copy-start.39
  308.2 5.7 copy-start.41
  308.2 5.7 copy-start.43
  308.2 5.7 copy-start.45
  308.2 5.7 copy-start.47
  308.2 5.7 copy-start.49
  308.2 5.7 copy-start.51
  308.2 5.7 copy-start.53
  308.3 5.7 copy-start.55
  308.3 5.7 copy-start.57
  308.3 5.7 copy-start.59
  479.8 8.2 %collective-permute-start.5 = (f32[3,32,1,8,128]{4,1,3,2,0:T(8,128)S(1)}, f32[3,32,1,8,128]{4,1,3,2,0:T(8,128)S(1)}, u32[]{:S(2)}, u32[]{:S(2)}) collective-permute-start(f32[3,32,1,8,128]{4,1,3,2,0:T(8,128)S(1)} %get-tuple-element.37), channel_id=1, source_target_pairs={{0,4},{4,8},{8,12},{12,16},{16,20},{20,24},{24,28},{28,32},{32,36}... | collective-permute-start | bytes 1179656 | tf_op jit(solution)/shard_map/ppermute | solution.py:18
  483.3 9.1 %collective-permute-start.6 = (f32[3,32,1,8,128]{4,1,3,2,0:T(8,128)S(1)}, f32[3,32,1,8,128]{4,1,3,2,0:T(8,128)S(1)}, u32[]{:S(2)}, u32[]{:S(2)}) collective-permute-start(f32[3,32,1,8,128]{4,1,3,2,0:T(8,128)S(1)} %get-tuple-element.38), channel_id=1, source_target_pairs={{4,0},{8,4},{12,8},{16,12},{20,16},{24,20},{28,24},{32,28},{36,32}... | collective-permute-start | bytes 1179656 | tf_op jit(solution)/shard_map/ppermute | solution.py:20
  501.1 8.2 %collective-permute-start.7 = (f32[3072]{0:T(1024)}, f32[3072]{0:T(1024)}, u32[]{:S(2)}, u32[]{:S(2)}) collective-permute-start(f32[3072]{0:T(1024)} %reshape_squeeze.14), channel_id=1, source_target_pairs={{0,1},{1,2},{2,3},{3,0},{4,5},{5,6},{6,7},{7,4},{8,9},{9,10},{10,1... | collective-permute-start | bytes 36872 | tf_op jit(solution)/shard_map/ppermute | solution.py:30
  506.0 8.1 %collective-permute-start.8 = (f32[3072]{0:T(1024)}, f32[3072]{0:T(1024)}, u32[]{:S(2)}, u32[]{:S(2)}) collective-permute-start(f32[3072]{0:T(1024)} %reshape_squeeze.15), channel_id=1, source_target_pairs={{0,3},{1,0},{2,1},{3,2},{4,7},{5,4},{6,5},{7,6},{8,11},{9,8},{10,9... | collective-permute-start | bytes 36872 | tf_op jit(solution)/shard_map/ppermute | solution.py:30
  532.2 159.4 %copy-start.18 = (f32[1,32,32]{1,2,0:T(8,128)S(1)}, f32[1,32,32]{1,2,0:T(8,128)}, u32[]{:S(2)}) copy-start(f32[1,32,32]{1,2,0:T(8,128)} %get-tuple-element.84) | copy-start | bytes 12292
  532.2 159.4 %copy-start.19 = (f32[1,32,32]{1,2,0:T(8,128)S(1)}, f32[1,32,32]{1,2,0:T(8,128)}, u32[]{:S(2)}) copy-start(f32[1,32,32]{1,2,0:T(8,128)} %get-tuple-element.86) | copy-start | bytes 12292
  532.2 160.2 %copy-start.20 = (f32[1,32,32]{1,2,0:T(8,128)S(1)}, f32[1,32,32]{1,2,0:T(8,128)}, u32[]{:S(2)}) copy-start(f32[1,32,32]{1,2,0:T(8,128)} %multiply_bitcast_fusion.2) | copy-start | bytes 12292
  532.2 165.7 %copy-start.1 = (f32[16]{0:T(128)S(1)}, f32[16]{0:T(128)}, u32[]{:S(2)}) copy-start(f32[16]{0:T(128)} %param.22) | copy-start | bytes 196
  (53 other events, 197.1 us)
Sparse Core Ops, SparseCore 0:
  135.3 112.6 all-gather.1
where the time goes:
time: 713 us; the launch traced here: 705 us
  blocking collectives  389 us (55%)
  matrix products  117 us (16%)
  local copies, waits for them, and re-layouts  112 us (16%)
  other arithmetic  37.7 us (5%)
  starting transfers between devices  18 us (3%)
  between operations  15.9 us (2%)
  waiting for transfers between devices  15.2 us (2%)
    psum x2, blocking collectives, advance(): lax.psum(local_inner(basis_block, image_block), ('slab', 'dom')) / dof_count  160 us
    psum x2, blocking collectives, advance(): lax.psum(local_inner(residual, residual), ('slab', 'dom')) / dof_count  147 us
    psum x1, blocking collectives, per_device(): lax.psum(local_inner(start_block, start_block), ('slab', 'dom')) / dof_count  82.3 us
    dot_general x1, matrix products, element_matrices(): jnp.einsum('ia...,ib...->ab...', gradients, pushed, precision=highest)  57.4 us
    dot_general x1, matrix products, element_matrices(): jnp.einsum('ik...,kb...->ib...', stress_matrix(stress), gradients, precis...  39.3 us
    gather x2, local copies, waits for them, and re-layouts, per_device(): jnp.take(shard_piece, jnp.clip(flat_columns, 0, shard_piece.shape[1] - 1)...  35.7 us
  transfers between devices with their start and end apart: 10, of which 5 were waited for; matrix products, arithmetic and copies ran while one was open for 6% of the time, Pallas kernels for 0%

commit v1 on v0

--- a/solution.py
+++ b/solution.py
@@ -142,7 +142,10 @@
 
 
 def advance(basis_block, image_block, dof_count):
-    projection = lax.psum(local_inner(basis_block, image_block), ("slab", "dom")) / dof_count
+    projection = (
+        jnp.sum(lax.all_gather(local_inner(basis_block, image_block), ("slab", "dom")), axis=0)
+        / dof_count
+    )
     residual = image_block - mix(basis_block, projection)
     gram_matrix = lax.psum(local_inner(residual, residual), ("slab", "dom")) / dof_count
     following, upper_factor = normalize(residual, gram_matrix)

time: 713 us -> 793 us (1.11)
  waiting for transfers between devices: 15.2 us -> 248 us
  blocking collectives: 389 us -> 232 us
    all_gather x0 -> x2, waiting for transfers between devices: none -> 232 us  [advance(): lax.all_gather(local_inner(basis_block, image_block), ('slab', 'dom'))]
    psum x2 -> x0, blocking collectives: 160 us -> none  [advance(): lax.psum(local_inner(basis_block, image_block), ('slab', 'dom')) / dof_count]
  transfers between devices with their start and end apart: 10 -> 12, of which waited for: 5 -> 7; matrix products, arithmetic and copies ran while one was open for 6% -> 5% of each run, Pallas kernels for 0% -> 0%
where the time goes in v1:
time: 793 us; the launch traced here: 786 us
  waiting for transfers between devices  248 us (31%)
  blocking collectives  232 us (29%)
  matrix products  118 us (15%)
  local copies, waits for them, and re-layouts  113 us (14%)
  other arithmetic  42.8 us (5%)
  starting transfers between devices  17.3 us (2%)
  between operations  15.6 us (2%)
    all_gather x2, waiting for transfers between devices, advance(): lax.all_gather(local_inner(basis_block, image_block), ('slab', 'dom'))  232 us
    psum x2, blocking collectives, advance(): lax.psum(local_inner(residual, residual), ('slab', 'dom')) / dof_count  150 us
    psum x1, blocking collectives, per_device(): lax.psum(local_inner(start_block, start_block), ('slab', 'dom')) / dof_count  82.3 us
    dot_general x1, matrix products, element_matrices(): jnp.einsum('ia...,ib...->ab...', gradients, pushed, precision=highest)  57.6 us
    dot_general x1, matrix products, element_matrices(): jnp.einsum('ik...,kb...->ib...', stress_matrix(stress), gradients, precis...  39.3 us
    gather x2, local copies, waits for them, and re-layouts, per_device(): jnp.take(shard_piece, jnp.clip(flat_columns, 0, shard_piece.shape[1] - 1)...  35.6 us
  transfers between devices with their start and end apart: 12, of which 7 were waited for; matrix products, arithmetic and copies ran while one was open for 5% of the time, Pallas kernels for 0%

profile of v1, /device:TPU:1, one launch (start us, length us, event | category | flops | bytes accessed | tf_op | source)
XLA Modules:
  0.0 785.6 jit_solution(7153947441334769789)
XLA Ops:
  9.1 7.5 copy.177
  16.7 7.2 copy.178
  23.9 39.3 %fusion.144 = f32[5376,3,8]{2,1,0:T(4,128)S(1)} fusion(f32[3,3,5376]{1,0,2:T(4,128)} %copy.177, f32[3,8,5376]{1,0,2:T(4,128)} %copy.178), kind=kOutput, calls=%fused_computation.282 | convolution fusion | flops 4644864 | bytes 1225728 | tf_op jit(solution)/shard_map/ik...,kb...->ib.../dot_general | solution.py:71
  63.5 57.6 %multiply_bitcast_fusion = f32[8,8,5376]{0,1,2:T(8,128)} fusion(f32[5376]{0:T(1024)S(1)} %convolution_reduce_fusion, f32[3,8,5376]{1,0,2:T(4,128)S(1)} %copy-done.2, f32[5376,3,8]{2,1,0:T(4,128)S(1)} %fusion.144), kind=kOutput, calls=%fused_computation.1 | convolution fusion | flops 12730368 | bytes 2429952 | tf_op jit(solution)/shard_map/ia...,ib...->ab.../dot_general | solution.py:72
  121.1 12.2 %copy.180 = f32[8,8,5376]{2,1,0:T(8,128)S(1)} copy(f32[8,8,5376]{0,1,2:T(8,128)} %multiply_bitcast_fusion) | data formatting | bytes 2752512 | tf_op jit(solution)/shard_map/mul | solution.py:72
  133.3 2.1 copy.181
  136.5 82.3 %psum.21 = f32[32,32]{0,1:T(8,128)S(1)} all-reduce(f32[32,32]{0,1:T(8,128)S(1)} %convolution_bitcast_fusion.10), channel_id=1, replica_groups=mesh['slab'=64,'dom'=4] {'slab','dom'}, use_global_device_ids=true, to_apply=%region_0.0 | all-reduce | flops 1024 | bytes 8192 | tf_op jit(solution)/shard_map/psum | solution.py:192
  218.9 2.9 cholesky.59
  223.7 2.4 custom-call.7
  227.4 2.1 collective-permute-start.1
  229.6 2.4 collective-permute-start.2
  234.3 4.8 collective-permute-done.2
  239.2 1.7 fusion.137
  240.9 3.8 copy.195
  245.2 2.4 copy.196
  247.9 2.4 collective-permute-start.4
  251.2 2.3 copy.197
  253.8 3.5 copy.198
  257.2 4.5 select_maximum_fusion.4
  261.8 31.8 %gather_fusion = f32[8192,64]{1,0:T(8,128)} fusion(f32[64,21504]{0,1:T(8,128)} %all-gather.6.cloned.1.call-done, s32[8192]{0:T(1024)S(1)} %copy-done.15), kind=kCustom, calls=%fused_computation | custom fusion | bytes 4227072 | tf_op jit(solution)/shard_map/jit(_take)/gather | solution.py:174
  293.6 3.8 copy.182
  297.4 2.0 copy.244
  301.7 2.3 collective-permute-start
  305.3 2.7 collective-permute-done
  308.8 5.4 fusion.41
  315.9 117.9 %all-gather.8.cloned.1.call-done = f32[8192,32]{1,0:T(8,128)} async-done(((f32[32,32]{1,0:T(8,128)}), f32[8192,32]{1,0:T(8,128)}) %all-gather.8.cloned.1.call-update) | async-done | bytes 1048592 | tf_op jit(solution)/shard_map/all_gather | solution.py:146
  433.8 2.5 reduce_sum.38
  438.0 74.9 %psum.22 = f32[32,32]{0,1:T(8,128)S(1)} all-reduce(f32[32,32]{0,1:T(8,128)S(1)} %convolution_bitcast_fusion.8), channel_id=1, replica_groups=mesh['slab'=64,'dom'=4] {'slab','dom'}, use_global_device_ids=true, to_apply=%region_7.10 | all-reduce | flops 1024 | bytes 8192 | tf_op jit(solution)/shard_map/psum | solution.py:150
  512.9 2.9 cholesky.70
  517.7 2.4 custom-call.8
  521.3 2.7 collective-permute-start.5
  524.0 1.9 collective-permute-start.6
  525.9 2.8 collective-permute-done.5
  528.7 4.4 collective-permute-done.6
  535.7 4.4 copy.204
  540.1 1.7 reshape_squeeze.14
  542.0 3.1 copy.205
  545.1 1.7 reshape_squeeze.15
  546.8 2.7 collective-permute-start.8
  551.1 3.2 copy.206
  556.0 4.4 copy.207
  560.6 3.4 select_maximum_fusion
  564.3 7.2 fusion.10
  574.5 114.4 %all-gather.10.cloned.1.call-done = f32[8192,32]{1,0:T(8,128)} async-done(((f32[32,32]{1,0:T(8,128)}), f32[8192,32]{1,0:T(8,128)}) %all-gather.10.cloned.1.call-update) | async-done | bytes 1048592 | tf_op jit(solution)/shard_map/all_gather | solution.py:146
  689.0 2.6 reduce_sum.39
  693.2 75.1 %psum.23 = f32[32,32]{0,1:T(8,128)S(1)} all-reduce(f32[32,32]{0,1:T(8,128)S(1)} %convolution_bitcast_fusion.6), channel_id=1, replica_groups=mesh['slab'=64,'dom'=4] {'slab','dom'}, use_global_device_ids=true, to_apply=%region_9.12 | all-reduce | flops 1024 | bytes 8192 | tf_op jit(solution)/shard_map/psum | solution.py:150
  768.4 2.9 cholesky.81
  774.1 2.4 custom-call.9
  (276 shorter events, 36.7 us)
Async XLA Ops:
  7.2 56.1 %copy-start = (f32[16]{0:T(128)S(1)}, f32[16]{0:T(128)}, u32[]{:S(2)}) copy-start(f32[16]{0:T(128)} %param.22) | copy-start | bytes 196
  7.2 254.6 %all-gather.6.cloned.1.call-start = ((), (), s32[]{:S(2)}) async-start(), calls=%async_computation | async-start | bytes 13762560 | tf_op jit(solution)/shard_map/all_gather | solution.py:172
  9.1 7.5 copy-start.13
  23.9 39.3 %copy-start.89 = (s32[5376]{0:T(1024)S(1)}, s32[5376]{0:T(1024)}, u32[]{:S(2)}) copy-start(s32[5376]{0:T(1024)} %param.21) | copy-start | bytes 64516
  23.9 39.6 %copy-start.2 = (f32[3,8,5376]{1,0,2:T(4,128)S(1)}, f32[3,8,5376]{1,0,2:T(4,128)}, u32[]{:S(2)}) copy-start(f32[3,8,5376]{1,0,2:T(4,128)} %copy.178) | copy-start | bytes 1548292
  135.5 96.5 %copy-start.90 = (s32[1,4]{1,0:T(1,128)S(1)}, s32[1,4]{1,0:T(1,128)}, u32[]{:S(2)}) copy-start(s32[1,4]{1,0:T(1,128)} %param.23) | copy-start | bytes 52
  135.5 96.8 %copy-start.16 = (s32[4,2,8,128]{3,2,1,0:T(8,128)S(1)}, s32[4,2,8,128]{3,2,1,0:T(8,128)}, u32[]{:S(2)}) copy-start(s32[4,2,8,128]{3,2,1,0:T(8,128)} %param.24) | copy-start | bytes 98308
  135.5 298.3 %all-gather.8.cloned.1.call-start = ((), (), s32[]{:S(2)}) async-start(), calls=%async_computation.1 | async-start | bytes 4210688 | tf_op jit(solution)/shard_map/all_gather | solution.py:146
  227.4 6.8 collective-permute-start.1
  229.6 9.5 %collective-permute-start.2 = (f32[3,32,1,8,128]{4,1,3,2,0:T(8,128)S(1)}, f32[3,32,1,8,128]{4,1,3,2,0:T(8,128)S(1)}, u32[]{:S(2)}, u32[]{:S(2)}) collective-permute-start(f32[3,32,1,8,128]{4,1,3,2,0:T(8,128)S(1)} %get-tuple-element.43), channel_id=1, source_target_pairs={{4,0},{8,4},{12,8},{16,12},{20,16},{24,20},{28,24},{32,28},{36,32}... | collective-permute-start | bytes 1179656 | tf_op jit(solution)/shard_map/ppermute | solution.py:20
  239.1 18.2 %copy-start.6 = (f32[3,32,1,8,128]{4,1,3,2,0:T(8,128)}, f32[3,32,1,8,128]{4,1,3,2,0:T(8,128)S(1)}, u32[]{:S(2)}) copy-start(f32[3,32,1,8,128]{4,1,3,2,0:T(8,128)S(1)} %collective-permute-done.2) | copy-start | bytes 1179652
  239.2 11.1 %copy-start.17 = (f32[4,2,8,128]{3,2,1,0:T(8,128)S(1)}, f32[4,2,8,128]{3,2,1,0:T(8,128)}, u32[]{:S(2)}) copy-start(f32[4,2,8,128]{3,2,1,0:T(8,128)} %get-tuple-element.83) | copy-start | bytes 98308
  244.9 6.1 collective-permute-start.3
  247.9 5.6 collective-permute-start.4
  293.6 5.9 copy-start.78
  299.5 8.4 %copy-start.81 = (f32[8,27,1,1]{1,0,3,2:T(8,128)S(1)}, f32[8,27,1,1]{1,0,3,2:T(8,128)}, u32[]{:S(2)}) copy-start(f32[8,27,1,1]{1,0,3,2:T(8,128)} %constant.100) | copy-start | bytes 2596
  299.8 9.0 %copy-start.3 = (f32[3,32,4,10,130]{4,1,3,2,0:T(8,128)S(1)}, f32[3,32,4,10,130]{4,1,3,2,0:T(8,128)}, u32[]{:S(2)}) copy-start(f32[3,32,4,10,130]{4,1,3,2,0:T(8,128)} %select_maximum_fusion.4) | copy-start | bytes 5990404
  299.8 9.0 %copy-start.4 = (f32[3,32,4,8,1]{4,1,3,2,0:T(8,128)S(1)}, f32[3,32,4,8,1]{4,1,3,2,0:T(8,128)}, u32[]{:S(2)}) copy-start(f32[3,32,4,8,1]{4,1,3,2,0:T(8,128)} %copy.198) | copy-start | bytes 36868
  299.8 9.0 %copy-start.7 = (f32[3,32,1,8,128]{4,1,3,2,0:T(8,128)S(1)}, f32[3,32,1,8,128]{4,1,3,2,0:T(8,128)}, u32[]{:S(2)}) copy-start(f32[3,32,1,8,128]{4,1,3,2,0:T(8,128)} %copy-done.6) | copy-start | bytes 1179652
  299.8 9.0 %copy-start.79 = (f32[3,2,8,128]{3,2,1,0:T(8,128)S(1)}, f32[3,2,8,128]{3,2,1,0:T(8,128)}, u32[]{:S(2)}) copy-start(f32[3,2,8,128]{3,2,1,0:T(8,128)} %param.25) | copy-start | bytes 73732
  301.7 6.3 collective-permute-start
  308.5 5.7 copy-start.22
  308.5 5.7 copy-start.24
  308.5 5.7 copy-start.26
  308.5 5.7 copy-start.28
  308.5 5.7 copy-start.30
  308.5 5.7 copy-start.32
  308.5 5.7 copy-start.34
  308.6 5.7 copy-start.36
  308.6 5.7 copy-start.38
  308.6 5.7 copy-start.40
  308.6 5.7 copy-start.42
  308.6 5.7 copy-start.44
  308.6 5.7 copy-start.46
  308.6 5.7 copy-start.48
  308.6 5.7 copy-start.50
  308.6 5.7 copy-start.52
  308.6 5.7 copy-start.54
  315.9 373.1 %all-gather.10.cloned.1.call-start = ((), (), s32[]{:S(2)}) async-start(), calls=%async_computation.2 | async-start | bytes 4210688 | tf_op jit(solution)/shard_map/all_gather | solution.py:146
  436.4 83.7 %copy-start.14 = (f32[32,32]{0,1:T(8,128)}, f32[32,32]{0,1:T(8,128)S(1)}, u32[]{:S(2)}) copy-start(f32[32,32]{0,1:T(8,128)S(1)} %copy.201) | copy-start | bytes 12292
  521.3 7.4 collective-permute-start.5
  524.0 9.1 %collective-permute-start.6 = (f32[3,32,1,8,128]{4,1,3,2,0:T(8,128)S(1)}, f32[3,32,1,8,128]{4,1,3,2,0:T(8,128)S(1)}, u32[]{:S(2)}, u32[]{:S(2)}) collective-permute-start(f32[3,32,1,8,128]{4,1,3,2,0:T(8,128)S(1)} %get-tuple-element.41), channel_id=1, source_target_pairs={{4,0},{8,4},{12,8},{16,12},{20,16},{24,20},{28,24},{32,28},{36,32}... | collective-permute-start | bytes 1179656 | tf_op jit(solution)/shard_map/ppermute | solution.py:20
  541.8 7.6 collective-permute-start.7
  546.8 7.5 collective-permute-start.8
  573.7 117.9 %copy-start.10 = (f32[3,32,2,8,128]{4,1,3,2,0:T(8,128)S(1)}, f32[3,32,2,8,128]{4,1,3,2,0:T(8,128)}, u32[]{:S(2)}) copy-start(f32[3,32,2,8,128]{4,1,3,2,0:T(8,128)} %copy-done.9) | copy-start | bytes 2359300
  689.0 83.6 %copy-start.20 = (f32[1,32,32]{1,2,0:T(8,128)S(1)}, f32[1,32,32]{1,2,0:T(8,128)}, u32[]{:S(2)}) copy-start(f32[1,32,32]{1,2,0:T(8,128)} %get-tuple-element.87) | copy-start | bytes 12292
  689.0 83.6 %copy-start.21 = (f32[1,32,32]{1,2,0:T(8,128)S(1)}, f32[1,32,32]{1,2,0:T(8,128)}, u32[]{:S(2)}) copy-start(f32[1,32,32]{1,2,0:T(8,128)} %get-tuple-element.89) | copy-start | bytes 12292
  689.0 89.9 %copy-start.1 = (f32[16]{0:T(128)S(1)}, f32[16]{0:T(128)}, u32[]{:S(2)}) copy-start(f32[16]{0:T(128)} %param.22) | copy-start | bytes 196
  (55 other events, 207.7 us)
Sparse Core Ops, SparseCore 0:
  135.6 112.6 all-gather.5
  316.0 117.7 all-gather.7
  573.9 115.0 all-gather.9
